TPU v7x, 256 devices: a whole 4x4x8 slice. The times are simulated.
256 devices in a mesh: dp: 4 (over y), tensor: 64 (over x, z, core).
Axes of the slice: x: 4, y: 4, z: 8, core: 2. Of those that a mesh axis runs over, the one named last changes fastest.
Arguments:
- tokens: bfloat16 [4, 8192, 1536], P('dp', 'tensor'), may hold values from -6 to 6
- attn_gain: float32 [1536], replicated, may hold values from 0.1 to 1.9
- qkv_weight: bfloat16 [1536, 2560], P(None, 'dp'), may hold values from -0.25 to 0.25
- out_weight: bfloat16 [1536, 1536], P('dp'), may hold values from -0.15625 to 0.15625
- prefix_cache: bfloat16 [4, 512, 2, 512], P('dp', 'tensor'), may hold values from -640 to 640
- lengths: int32 [4, 256], P('dp'), may hold values from 1 to 384, 8192 in all within a row
- ffn_gain: float32 [1536], replicated, may hold values from 0.1 to 1.9
- expert_ids: int32 [4, 8192, 8], P('dp', 'tensor'), may hold values from 0 to 31, all different within a row; in each aligned block of 128 rows (0 to 127, 128 to 255, ..., all dimensions but the last counted through in order) at most 40 rows name the same one
- gate_weights: float32 [4, 8192, 8], P('dp', 'tensor'), may hold values from 0.05 to 0.5
- expert_in: bfloat16 [64, 1536, 512], P('tensor'), may hold values from -0.15625 to 0.15625
- expert_out: bfloat16 [64, 256, 1536], P('tensor'), may hold values from -0.25 to 0.25
Outputs:
- hidden_state: bfloat16 [4, 8192, 1536], P('dp', 'tensor')
- mixed: bfloat16 [4, 8192, 1536], P('dp', 'tensor')
Inputs may be any that keep to these rules, and one draw needn't show every extreme that they name: `lengths`: each group's 256 requests fill its 8192 suffix positions in order, and the longest holds exactly 384 tokens. `expert_ids`: each token names 8 different experts; among the 128 tokens of one device no expert is named more than 40 times, a bound that some block reaches.
All inputs are finite; a program needn't handle non-finite values.
Results may differ from a plain program's by a relative error of at most 0.014.
The roundings to bfloat16 on the way count: a program that leaves them out, or rounds other values in their place, can miss the bound.
Values may be sent and summed in bfloat16 or wider, within the bound.
No kernel may reach another device: no remote copies, remote signals or barrier semaphores. Data moves between devices by JAX's collectives and lax.ppermute only.
A program may use at most 128 MiB of HBM per device.

v0:
```python
import jax
import jax.numpy as jnp
from jax import lax
from jax.sharding import PartitionSpec as P

HEADS = 24
KV_HEADS = 8
HEAD_DIM = 64
EXPERTS = 32
TOPK = 8
SHIFTS = 2
CAP = 40
TENSOR = ("chip", "core")
EPS = 1e-06
THETA = 10000.0


def from_behind(value, axis, steps):
    count = lax.axis_size(axis)
    first, last = (max(0, -steps), min(count, count - steps))
    return lax.ppermute(value, axis, [(source, source + steps) for source in range(first, last)])


def rms_norm(x, gain):
    values = x.astype(jnp.float32)
    mean_sq = jnp.mean(values * values, axis=-1, keepdims=True)
    return (values * lax.rsqrt(mean_sq + EPS) * gain).astype(jnp.bfloat16)


def rotary(x, positions):
    half = x.shape[-1] // 2
    freqs = THETA ** (-jnp.arange(half, dtype=jnp.float32) * 2.0 / x.shape[-1])
    angles = positions.astype(jnp.float32)[:, None] * freqs[None, :]
    cosine = jnp.concatenate([jnp.cos(angles), jnp.cos(angles)], axis=-1)[:, None, :]
    sine = jnp.concatenate([jnp.sin(angles), jnp.sin(angles)], axis=-1)[:, None, :]
    turned = jnp.concatenate([-x[..., half:], x[..., :half]], axis=-1)
    return x * cosine + turned * sine


def request_info(index, lengths):
    ends = jnp.cumsum(lengths, dtype=jnp.int32)
    before = ends[None, :] <= index[:, None]
    segment = jnp.sum(before.astype(jnp.int32), axis=1, dtype=jnp.int32)
    start = jnp.sum(jnp.where(before, lengths[None, :], 0), axis=1, dtype=jnp.int32)
    return (segment, index - start)


def merge_block(carry, scores, values, visible):
    best, total, acc = carry
    if visible is not None:
        scores = jnp.where(visible, scores, -1e30)
    newest = jnp.maximum(best, jnp.max(scores, axis=-1))
    probs = jnp.exp(scores - newest[..., None])
    if visible is not None:
        probs = jnp.where(visible, probs, 0.0)
    decay = jnp.exp(best - newest)
    total = total * decay + jnp.sum(probs, axis=-1)
    acc = acc * decay[..., None] + jnp.einsum(
        "tgrn,ngd->tgrd", probs.astype(jnp.bfloat16), values, preferred_element_type=jnp.float32
    )
    return (newest, total, acc)


def shards(
    tokens,
    attn_gain,
    qkv_weight,
    out_weight,
    prefix_cache,
    lengths,
    ffn_gain,
    expert_ids,
    gate_weights,
    expert_in,
    expert_out,
):
    rows = tokens.shape[1]
    model = tokens.shape[2]
    head_cols = HEADS * HEAD_DIM
    kv_cols = KV_HEADS * HEAD_DIM
    ratio = HEADS // KV_HEADS
    scale = 1.0 / HEAD_DIM**0.5
    lanes = lax.axis_size(TENSOR)
    prefix_len = prefix_cache.shape[1] * lanes
    own_lengths = lengths[0]
    inputs = tokens[0]
    normed = rms_norm(inputs, attn_gain)
    full_qkv, full_out = (
        lax.all_gather(qkv_weight, "dp", axis=1, tiled=True),
        lax.all_gather(out_weight, "dp", axis=0, tiled=True),
    )
    qkv = jnp.dot(normed, full_qkv, preferred_element_type=jnp.float32).astype(jnp.bfloat16)
    lane = lax.axis_index(TENSOR)
    q_index = lane * rows + jnp.arange(rows, dtype=jnp.int32)
    q_segment, offset = request_info(q_index, own_lengths)
    positions = prefix_len + offset
    query = rotary(
        qkv[:, :head_cols].astype(jnp.float32).reshape(rows, HEADS, HEAD_DIM), positions
    ).astype(jnp.bfloat16)
    query = query.reshape(rows, KV_HEADS, ratio, HEAD_DIM)
    keys = rotary(
        qkv[:, head_cols : head_cols + kv_cols]
        .astype(jnp.float32)
        .reshape(rows, KV_HEADS, HEAD_DIM),
        positions,
    ).astype(jnp.bfloat16)
    local_pairs = jnp.stack([keys.reshape(rows, kv_cols), qkv[:, head_cols + kv_cols :]], axis=1)
    start_carry = (
        jnp.full((rows, KV_HEADS, ratio), -1e30, jnp.float32),
        jnp.zeros((rows, KV_HEADS, ratio), jnp.float32),
        jnp.zeros((rows, KV_HEADS, ratio, HEAD_DIM), jnp.float32),
    )
    piece = lax.all_gather(prefix_cache[0], TENSOR, axis=0, tiled=True)
    count = piece.shape[0]
    cached_keys = piece[:, 0].reshape(count, KV_HEADS, HEAD_DIM)
    cached_values = piece[:, 1].reshape(count, KV_HEADS, HEAD_DIM)
    scores = (
        jnp.einsum("tgrd,ngd->tgrn", query, cached_keys, preferred_element_type=jnp.float32) * scale
    )
    carry = merge_block(start_carry, scores, cached_values, None)
    window = local_pairs[None]
    for bit in range(SHIFTS):
        earlier = from_behind(window, TENSOR, 2**bit)
        window = jnp.concatenate([window, earlier], axis=0)
    depth = window.shape[0]
    k_index = (
        (lane - jnp.arange(depth, dtype=jnp.int32))[:, None] * rows
        + jnp.arange(rows, dtype=jnp.int32)[None, :]
    ).reshape(-1)
    k_segment, unused = request_info(k_index, own_lengths)
    visible = (
        (k_index[None, :] >= 0)
        & (k_index[None, :] <= q_index[:, None])
        & (k_segment[None, :] == q_segment[:, None])
    )
    suffix_pairs = window.reshape(depth * rows, 2, kv_cols)
    suffix_keys = suffix_pairs[:, 0].reshape(depth * rows, KV_HEADS, HEAD_DIM)
    suffix_values = suffix_pairs[:, 1].reshape(depth * rows, KV_HEADS, HEAD_DIM)
    scores = (
        jnp.einsum("tgrd,ngd->tgrn", query, suffix_keys, preferred_element_type=jnp.float32) * scale
    )
    best, total, acc = merge_block(carry, scores, suffix_values, visible[:, None, None, :])
    attended = (acc / total[..., None]).astype(jnp.bfloat16).reshape(rows, head_cols)
    projected = jnp.dot(attended, full_out, preferred_element_type=jnp.float32)
    hidden_state = (inputs.astype(jnp.float32) + projected).astype(jnp.bfloat16)
    moe_input = rms_norm(hidden_state, ffn_gain)
    chips = lax.axis_size("chip")
    unit_ff = expert_in.shape[2] // 2
    flat_ids = expert_ids[0].reshape(-1)
    onehot = (flat_ids[:, None] == jnp.arange(EXPERTS, dtype=jnp.int32)[None, :]).astype(jnp.int32)
    earlier_count = jnp.cumsum(onehot, axis=0, dtype=jnp.int32) - onehot
    slots = jnp.sum(earlier_count * onehot, axis=1, dtype=jnp.int32)
    target = flat_ids * CAP + slots
    row_of = jnp.repeat(jnp.arange(rows, dtype=jnp.int32), TOPK)
    source = jnp.full((chips * CAP,), rows, jnp.int32).at[target].set(row_of)
    padded_input = jnp.concatenate([moe_input, jnp.zeros((1, model), jnp.bfloat16)], axis=0)
    outgoing = padded_input[source].reshape(chips, CAP, model)
    arrived = lax.all_to_all(outgoing, "chip", 0, 0, tiled=True)
    sibling = lax.ppermute(arrived, "core", [(0, 1), (1, 0)])
    unit_rows = jnp.concatenate([arrived, sibling], axis=0).reshape(2 * chips * CAP, model)
    inner = jnp.dot(unit_rows, expert_in[0], preferred_element_type=jnp.float32)
    activated = (jax.nn.silu(inner[:, :unit_ff]) * inner[:, unit_ff:]).astype(jnp.bfloat16)
    produced = jnp.dot(activated, expert_out[0], preferred_element_type=jnp.float32).astype(
        jnp.bfloat16
    )
    produced = produced.reshape(2, chips, CAP, model)
    partner = lax.ppermute(produced[1], "core", [(0, 1), (1, 0)])
    summed = (produced[0].astype(jnp.float32) + partner.astype(jnp.float32)).astype(jnp.bfloat16)
    returned = lax.all_to_all(summed, "chip", 0, 0, tiled=True)
    picked = returned.reshape(chips * CAP, model)[target].reshape(rows, TOPK, model)
    combined = jnp.einsum("tk,tkd->td", gate_weights[0], picked.astype(jnp.float32))
    mixed = (hidden_state.astype(jnp.float32) + combined).astype(jnp.bfloat16)
    return (hidden_state[None], mixed[None])


def solution(mesh):
    groups, lanes = mesh.devices.shape
    chip_mesh = jax.sharding.Mesh(
        mesh.devices.reshape(groups, lanes // 2, 2), ("dp", "chip", "core")
    )
    in_specs = (
        P("dp", TENSOR, None),
        P(),
        P(None, "dp"),
        P("dp", None),
        P("dp", TENSOR, None, None),
        P("dp", None),
        P(),
        P("dp", TENSOR, None),
        P("dp", TENSOR, None),
        P(TENSOR, None, None),
        P(TENSOR, None, None),
    )
    out_specs = (P("dp", TENSOR, None), P("dp", TENSOR, None))
    return jax.shard_map(
        shards, mesh=chip_mesh, in_specs=in_specs, out_specs=out_specs, check_vma=False
    )
```

profile of v0, /device:TPU:34, one launch (start us, length us, event | category | flops | bytes accessed | tf_op | source)
XLA Modules:
  0.0 489.5 jit_solution(2247679255793934085)
XLA Ops:
  14.9 9.0 %reduce-window.19 = s32[32,8,128]{2,1,0:T(8,128)S(1)} reduce-window(s32[32,8,128]{2,1,0:T(8,128)S(1)} %fusion.64, s32[]{:T(128)} %constant.27.clone.1), window={size=1x1x128 pad=0_0x0_0x127_0}, to_apply=%region_11.12 | reduce-window | flops 4161536 | bytes 262148 | tf_op jit(solution)/shard_map/reduce-window.2
  24.7 4.3 scatter_custom_fusion
  30.9 57.8 %all-gather.9.cloned.1.call-done = bf16[1,512,2,512]{3,2,0,1:T(2,128)(2,1)} async-done(((bf16[1,8,2,512]{3,2,0,1:T(2,128)(2,1)}), bf16[1,512,2,512]{3,2,0,1:T(2,128)(2,1)}) %all-gather.9.cloned.1.call-update) | async-done | bytes 1048592 | tf_op jit(solution)/shard_map/all_gather | solution.py:113
  88.7 4.3 fusion.74
  92.9 3.5 copy.57
  96.4 3.5 copy.58
  99.9 71.2 %all-gather.5.cloned.1.call-done = bf16[1536,2560]{1,0:T(8,128)(2,1)} async-done(((bf16[1536,640]{1,0:T(8,128)(2,1)}), bf16[1536,2560]{1,0:T(8,128)(2,1)}) %all-gather.5.cloned.1.call-update) | async-done | bytes 7864336 | tf_op jit(solution)/shard_map/all_gather | solution.py:89
  171.1 4.5 convolution_convert_fusion.1
  177.5 1.9 collective-permute-start
  179.9 5.7 %collective-permute-done = bf16[1,128,2,512]{3,1,2,0:T(8,128)(2,1)} collective-permute-done((bf16[1,128,2,512]{3,1,2,0:T(8,128)(2,1)}, bf16[1,128,2,512]{3,1,2,0:T(8,128)(2,1)}, u32[]{:S(2)}, u32[]{:S(2)}) %collective-permute-start) | collective-permute-done | bytes 262176 | tf_op jit(solution)/shard_map/ppermute | solution.py:21
  186.7 3.6 collective-permute-start.1
  191.3 4.8 bitcast_reduce_fusion
  196.0 5.5 %collective-permute-done.1 = bf16[2,128,2,512]{3,1,2,0:T(8,128)(2,1)S(1)} collective-permute-done((bf16[2,128,2,512]{3,1,2,0:T(8,128)(2,1)S(1)}, bf16[2,128,2,512]{3,1,2,0:T(8,128)(2,1)S(1)}, u32[]{:S(2)}, u32[]{:S(2)}) %collective-permute-start.1) | collective-permute-done | bytes 524320 | tf_op jit(solution)/shard_map/ppermute | solution.py:21
  205.1 2.1 copy.64
  208.3 3.7 fusion.3
  213.6 1.7 fusion.22
  216.6 1.7 fusion.40
  218.3 10.7 %all-gather.7.cloned.1.call-done = bf16[1536,1536]{1,0:T(8,128)(2,1)} async-done(((bf16[384,1536]{1,0:T(8,128)(2,1)}), bf16[1536,1536]{1,0:T(8,128)(2,1)}) %all-gather.7.cloned.1.call-update) | async-done | bytes 4718608 | tf_op jit(solution)/shard_map/all_gather | solution.py:90
  229.0 3.2 fusion.43
  232.5 5.4 %gather_fusion = bf16[1280,1536]{1,0:T(8,128)(2,1)} fusion(bf16[129,1536]{1,0:T(8,128)(2,1)S(1)} %concatenate.40, s32[2048]{0:T(1024)S(1)} %pad_clamp_fusion), kind=kCustom, calls=%fused_computation | custom fusion | bytes 7869440 | tf_op jit(solution)/shard_map/gather | solution.py:157
  237.9 99.6 %all_to_all.10 = bf16[32,40,1536]{2,1,0:T(8,128)(2,1)S(1)} all-to-all(bf16[32,40,1536]{2,1,0:T(8,128)(2,1)} %bitcast.159), channel_id=1, replica_groups=mesh['dp'=4,'chip'=32,'core'=2] {'chip'}, dimensions={0} | all-to-all | bytes 7864320 | tf_op jit(solution)/shard_map/all_to_all | solution.py:158
  337.5 2.0 copy-done.2
  339.5 6.9 %collective-permute-done.2 = bf16[32,40,1536]{2,1,0:T(8,128)(2,1)} collective-permute-done((bf16[32,40,1536]{2,1,0:T(8,128)(2,1)S(1)}, bf16[32,40,1536]{2,1,0:T(8,128)(2,1)}, u32[]{:S(2)}, u32[]{:S(2)}) %collective-permute-start.2) | collective-permute-done | bytes 3932192 | tf_op jit(solution)/shard_map/ppermute | solution.py:159
  346.4 7.1 %pad_maximum_fusion = bf16[64,40,1536]{2,1,0:T(8,128)(2,1)} fusion(bf16[32,40,1536]{2,1,0:T(8,128)(2,1)} %collective-permute-done.2, bf16[32,40,1536]{2,1,0:T(8,128)(2,1)} %copy-done.2), kind=kLoop, calls=%fused_computation.4 | loop fusion | flops 3932160 | bytes 15728640 | tf_op jit(solution)/shard_map/concatenate | solution.py:160
  353.4 6.6 %fusion.18 = f32[2560,512]{1,0:T(8,128)S(1)} fusion(bf16[2560,1536]{1,0:T(8,128)(2,1)} %bitcast.161, bf16[1,1536,512]{2,1,0:T(8,128)(2,1)S(1)} %copy-done), kind=kOutput, calls=%fused_computation.29 | convolution fusion | flops 4026531840 | bytes 14680064 | tf_op jit(solution)/shard_map/dot_general | solution.py:161
  360.1 2.3 convolution_convert_fusion
  363.1 6.7 %collective-permute-done.3 = bf16[32,40,1536]{2,1,0:T(8,128)(2,1)S(1)} collective-permute-done((bf16[32,40,1536]{2,1,0:T(8,128)(2,1)S(1)}, bf16[32,40,1536]{2,1,0:T(8,128)(2,1)S(1)}, u32[]{:S(2)}, u32[]{:S(2)}) %collective-permute-start.3) | collective-permute-done | bytes 3932192 | tf_op jit(solution)/shard_map/ppermute | solution.py:167
  369.8 3.0 fusion
  372.8 6.0 %all-to-all-start.1 = ((bf16[32,40,1536]{2,1,0:T(8,128)(2,1)}), bf16[32,40,1536]{2,1,0:T(8,128)(2,1)}, u32[]{:S(2)}, u32[]{:S(2)}) async-start(bf16[32,40,1536]{2,1,0:T(8,128)(2,1)} %fusion), calls=%async_computation.1 | async-start | bytes 7864320 | tf_op jit(solution)/shard_map/all_to_all | solution.py:169
  378.9 90.3 %all-to-all-done.1 = bf16[32,40,1536]{2,1,0:T(8,128)(2,1)} async-done(((bf16[32,40,1536]{2,1,0:T(8,128)(2,1)}), bf16[32,40,1536]{2,1,0:T(8,128)(2,1)}, u32[]{:S(2)}, u32[]{:S(2)}) %all-to-all-start.1) | async-done | bytes 3932192 | tf_op jit(solution)/shard_map/all_to_all | solution.py:169
  469.2 10.0 %gather_fusion.1 = bf16[1024,1536]{1,0:T(8,128)(2,1)} fusion(bf16[1280,1536]{1,0:T(8,128)(2,1)} %bitcast.47, s32[1024]{0:T(1024)S(1)} %broadcast_clamp_fusion), kind=kCustom, calls=%fused_computation.1 | custom fusion | bytes 6295552 | tf_op jit(solution)/shard_map/gather | solution.py:170
  479.2 2.8 fusion.9
  (104 shorter events, 24.0 us)
Async XLA Ops:
  7.2 346.3 %copy-start = (bf16[1,1536,512]{2,1,0:T(8,128)(2,1)S(1)}, bf16[1,1536,512]{2,1,0:T(8,128)(2,1)}, u32[]{:S(2)}) copy-start(bf16[1,1536,512]{2,1,0:T(8,128)(2,1)} %param.20) | copy-start | bytes 4718596
  7.2 81.5 %all-gather.9.cloned.1.call-start = ((), (), s32[]{:S(2)}) async-start(), calls=%async_computation.4 | async-start | bytes 1064960 | tf_op jit(solution)/shard_map/all_gather | solution.py:113
  7.9 163.2 %all-gather.5.cloned.1.call-start = ((), (), s32[]{:S(2)}) async-start(), calls=%async_computation.2 | async-start | bytes 9830400 | tf_op jit(solution)/shard_map/all_gather | solution.py:89
  8.7 162.5 %copy-start.3 = (bf16[1,128,1536]{2,1,0:T(8,128)(2,1)S(1)}, bf16[1,128,1536]{2,1,0:T(8,128)(2,1)}, u32[]{:S(2)}) copy-start(bf16[1,128,1536]{2,1,0:T(8,128)(2,1)} %param.11) | copy-start | bytes 1179652
  8.7 162.4 %copy-start.9 = (f32[1536]{0:T(1024)S(1)}, f32[1536]{0:T(1024)}, u32[]{:S(2)}) copy-start(f32[1536]{0:T(1024)} %param.12) | copy-start | bytes 18436
  8.7 220.3 %all-gather.7.cloned.1.call-start = ((), (), s32[]{:S(2)}) async-start(), calls=%async_computation.3 | async-start | bytes 5898240 | tf_op jit(solution)/shard_map/all_gather | solution.py:90
  30.7 69.2 %copy-start.8 = (f32[128,64]{0,1:T(8,128)}, f32[128,64]{0,1:T(8,128)S(1)}, u32[]{:S(2)}) copy-start(f32[128,64]{0,1:T(8,128)S(1)} %get-tuple-element.29) | copy-start | bytes 98308
  177.5 8.0 %collective-permute-start = (bf16[1,128,2,512]{3,1,2,0:T(8,128)(2,1)}, bf16[1,128,2,512]{3,1,2,0:T(8,128)(2,1)}, u32[]{:S(2)}, u32[]{:S(2)}) collective-permute-start(bf16[1,128,2,512]{3,1,2,0:T(8,128)(2,1)} %maximum_bitcast_fusion), channel_id=1, source_target_pairs={{0,1},{1,2},{2,3},{3,4},{4,5},{5,6},{6,7},{7,8},{8,9},{9,10},{10,1... | collective-permute-start | bytes 786440 | tf_op jit(solution)/shard_map/ppermute | solution.py:21
  186.7 14.9 %collective-permute-start.1 = (bf16[2,128,2,512]{3,1,2,0:T(8,128)(2,1)S(1)}, bf16[2,128,2,512]{3,1,2,0:T(8,128)(2,1)S(1)}, u32[]{:S(2)}, u32[]{:S(2)}) collective-permute-start(bf16[2,128,2,512]{3,1,2,0:T(8,128)(2,1)S(1)} %pad_maximum_fusion.2), channel_id=1, source_target_pairs={{0,2},{1,3},{2,4},{3,5},{4,6},{5,7},{6,8},{7,9},{8,10},{9,11},{10,... | collective-permute-start | bytes 1572872 | tf_op jit(solution)/shard_map/ppermute | solution.py:21
  191.2 16.0 %copy-start.5 = (pred[128,512]{0,1:T(8,128)(4,1)S(1)}, pred[128,512]{0,1:T(8,128)(4,1)}, u32[]{:S(2)}) copy-start(pred[128,512]{0,1:T(8,128)(4,1)} %compare_and_fusion) | copy-start | bytes 196612
  208.3 5.2 %copy-start.7 = (bf16[512,1,512]{0,2,1:T(8,128)(2,1)S(1)}, bf16[512,1,512]{0,2,1:T(8,128)(2,1)}, u32[]{:S(2)}) copy-start(bf16[512,1,512]{0,2,1:T(8,128)(2,1)} %copy.64) | copy-start | bytes 1572868
  213.5 2.4 slice-start
  213.5 2.4 copy-start.6
  213.6 3.1 slice-start.1
  216.6 15.6 %copy-start.10 = (f32[1536]{0:T(1024)S(1)}, f32[1536]{0:T(1024)}, u32[]{:S(2)}) copy-start(f32[1536]{0:T(1024)} %param.17) | copy-start | bytes 18436
  232.2 249.9 %copy-start.4 = (bf16[128,1536]{1,0:T(8,128)(2,1)}, bf16[128,1536]{1,0:T(8,128)(2,1)S(1)}, u32[]{:S(2)}) copy-start(bf16[128,1536]{1,0:T(8,128)(2,1)S(1)} %get-tuple-element.28) | copy-start | bytes 1179652
  337.5 2.0 copy-start.2
  339.5 6.9 %collective-permute-start.2 = (bf16[32,40,1536]{2,1,0:T(8,128)(2,1)S(1)}, bf16[32,40,1536]{2,1,0:T(8,128)(2,1)}, u32[]{:S(2)}, u32[]{:S(2)}) collective-permute-start(bf16[32,40,1536]{2,1,0:T(8,128)(2,1)S(1)} %all_to_all.10), channel_id=1, source_target_pairs={{0,1},{1,0},{2,3},{3,2},{4,5},{5,4},{6,7},{7,6},{8,9},{9,8},{10,11... | collective-permute-start | bytes 11796488 | tf_op jit(solution)/shard_map/ppermute | solution.py:159
  353.4 6.6 %copy-start.12 = (bf16[1,256,1536]{2,1,0:T(8,128)(2,1)S(1)}, bf16[1,256,1536]{2,1,0:T(8,128)(2,1)}, u32[]{:S(2)}) copy-start(bf16[1,256,1536]{2,1,0:T(8,128)(2,1)} %param.21) | copy-start | bytes 2359300
  362.9 6.9 %collective-permute-start.3 = (bf16[32,40,1536]{2,1,0:T(8,128)(2,1)S(1)}, bf16[32,40,1536]{2,1,0:T(8,128)(2,1)S(1)}, u32[]{:S(2)}, u32[]{:S(2)}) collective-permute-start(bf16[32,40,1536]{2,1,0:T(8,128)(2,1)S(1)} %bitcast.166), channel_id=1, source_target_pairs={{0,1},{1,0},{2,3},{3,2},{4,5},{5,4},{6,7},{7,6},{8,9},{9,8},{10,11... | collective-permute-start | bytes 11796488 | tf_op jit(solution)/shard_map/ppermute | solution.py:167
  372.8 6.0 %copy-start.11 = (f32[1,128,8]{1,2,0:T(8,128)S(1)}, f32[1,128,8]{1,2,0:T(8,128)}, u32[]{:S(2)}) copy-start(f32[1,128,8]{1,2,0:T(8,128)} %param.19) | copy-start | bytes 12292
  372.8 96.5 %all-to-all-start.1 = ((bf16[32,40,1536]{2,1,0:T(8,128)(2,1)}), bf16[32,40,1536]{2,1,0:T(8,128)(2,1)}, u32[]{:S(2)}, u32[]{:S(2)}) async-start(bf16[32,40,1536]{2,1,0:T(8,128)(2,1)} %fusion), calls=%async_computation.1 | async-start | bytes 7864320 | tf_op jit(solution)/shard_map/all_to_all | solution.py:169
  469.2 13.7 %copy-start.1 = (bf16[1,1536,512]{2,1,0:T(8,128)(2,1)S(1)}, bf16[1,1536,512]{2,1,0:T(8,128)(2,1)}, u32[]{:S(2)}) copy-start(bf16[1,1536,512]{2,1,0:T(8,128)(2,1)} %param.20) | copy-start | bytes 4718596
Sparse Core Ops, SparseCore 0:
  10.8 77.8 all-gather.8
  90.5 80.5 all-gather.4
  172.9 56.0 all-gather.6
where the time goes:
time: 490 us; the launch traced here: 489 us
  waiting for transfers between devices  257 us (52%)
  blocking collectives  99.6 us (20%)
  local copies, waits for them, and re-layouts  42 us (9%)
  other arithmetic  36.3 us (7%)
  matrix products  28.7 us (6%)
  between operations  14.2 us (3%)
  starting transfers between devices  11.9 us (2%)
    all_to_all x1, blocking collectives, shards(): arrived = lax.all_to_all(outgoing, 'chip', 0, 0, tiled=True)  99.6 us
    all_to_all x1, waiting for transfers between devices, shards(): returned = lax.all_to_all(summed, 'chip', 0, 0, tiled=True)  90.3 us
    all_gather x1, waiting for transfers between devices, shards(): lax.all_gather(qkv_weight, 'dp', axis=1, tiled=True)  71.2 us
    all_gather x1, waiting for transfers between devices, shards(): piece = lax.all_gather(prefix_cache[0], TENSOR, axis=0, tiled=True)  57.8 us
    ppermute x2, waiting for transfers between devices, from_behind(): lax.ppermute(value, axis, [(source, source + steps) for source in range(f...  11.2 us
    all_gather x1, waiting for transfers between devices, shards(): lax.all_gather(out_weight, 'dp', axis=0, tiled=True)  10.7 us
    another operation x6, other arithmetic  10.2 us
    gather x1, local copies, waits for them, and re-layouts, shards(): returned.reshape(chips * CAP, model)[target].reshape(rows, TOPK, model)  10 us
  transfers between devices with their start and end apart: 8, of which 8 were waited for; matrix products, arithmetic and copies ran while one was open for 13% of the time, Pallas kernels for 0%

commit v1 on v0

--- a/solution.py
+++ b/solution.py
@@ -1,3 +1,4 @@
+import functools
 import jax
 import jax.numpy as jnp
 from jax import lax
@@ -13,6 +14,31 @@
 TENSOR = ("chip", "core")
 EPS = 1e-06
 THETA = 10000.0
+
+
+def orders_do(my_data, at_axis):
+    current_value = lax.psum(1, axis_name="dp")
+    mat_out, latest, new = (current_value, lax.axis_index("dp"), my_data.shape[at_axis])
+    chunks = [u * mat_out if k == at_axis else u for k, u in enumerate(my_data.shape)]
+    carry_out = jnp.zeros(chunks, my_data.dtype)
+    k_now = lax.dynamic_update_slice_in_dim(carry_out, my_data, latest * new, axis=at_axis)
+    y = h_now = my_data
+    for num in tuple(range(1, mat_out // 2 + 1)):
+        y = lax.ppermute(y, axis_name="dp", perm=[(k, (k + 1) % mat_out) for k in range(mat_out)])
+        k_now = lax.dynamic_update_slice_in_dim(
+            k_now, y, (latest - num) % mat_out * new, axis=at_axis
+        )
+        if 2 * num < mat_out:
+            h_now = lax.ppermute(
+                h_now, axis_name="dp", perm=[(k, (k - 1) % mat_out) for k in range(mat_out)]
+            )
+            k_now = lax.dynamic_update_slice_in_dim(
+                k_now, h_now, (latest + num) % mat_out * new, axis=at_axis
+            )
+    return k_now
+
+
+save_slots = functools.partial(orders_do, at_axis=0)
 
 
 def from_behind(value, axis, steps):
@@ -87,7 +113,7 @@
     normed = rms_norm(inputs, attn_gain)
     full_qkv, full_out = (
         lax.all_gather(qkv_weight, "dp", axis=1, tiled=True),
-        lax.all_gather(out_weight, "dp", axis=0, tiled=True),
+        save_slots(out_weight),
     )
     qkv = jnp.dot(normed, full_qkv, preferred_element_type=jnp.float32).astype(jnp.bfloat16)
     lane = lax.axis_index(TENSOR)

time: 490 us -> 476 us (0.971)
  waiting for transfers between devices: 257 us -> 231 us
  local copies, waits for them, and re-layouts: 42 us -> 51.3 us
    all_gather x1, waiting for transfers between devices: 57.8 us -> 40.8 us  [shards(): piece = lax.all_gather(prefix_cache[0], TENSOR, axis=0, tiled=True)]
    all_gather x1 -> x0, waiting for transfers between devices: 10.7 us -> none  [shards(): lax.all_gather(out_weight, 'dp', axis=0, tiled=True)]
    dynamic_update_slice x0 -> x4, local copies, waits for them, and re-layouts: none -> 9.54 us  [the longest x2 4.79 us: orders_do(): lax.dynamic_update_slice_in_dim(k_now, y, (latest - num) % mat_out * new,...]
    ppermute x0 -> x3, waiting for transfers between devices: none -> 5.59 us  [the longest x2 5.59 us: orders_do(): lax.ppermute(y, axis_name='dp', perm=[(k, (k + 1) % mat_out) for k in ran...]
  transfers between devices with their start and end apart: 8 -> 10, of which waited for: 8 -> 8; matrix products, arithmetic and copies ran while one was open for 13% -> 10% of each run, Pallas kernels for 0% -> 0%
where the time goes in v1:
time: 476 us; the launch traced here: 472 us
  waiting for transfers between devices  231 us (49%)
  blocking collectives  98.5 us (21%)
  local copies, waits for them, and re-layouts  51.3 us (11%)
  other arithmetic  33.2 us (7%)
  matrix products  27.7 us (6%)
  starting transfers between devices  15.4 us (3%)
  between operations  14.5 us (3%)
    all_to_all x1, blocking collectives, shards(): arrived = lax.all_to_all(outgoing, 'chip', 0, 0, tiled=True)  98.5 us
    all_to_all x1, waiting for transfers between devices, shards(): returned = lax.all_to_all(summed, 'chip', 0, 0, tiled=True)  88.7 us
    all_gather x1, waiting for transfers between devices, shards(): lax.all_gather(qkv_weight, 'dp', axis=1, tiled=True)  68.9 us
    all_gather x1, waiting for transfers between devices, shards(): piece = lax.all_gather(prefix_cache[0], TENSOR, axis=0, tiled=True)  40.8 us
    ppermute x2, waiting for transfers between devices, from_behind(): lax.ppermute(value, axis, [(source, source + steps) for source in range(f...  12.3 us
    another operation x6, other arithmetic  10.2 us
    gather x1, local copies, waits for them, and re-layouts, shards(): returned.reshape(chips * CAP, model)[target].reshape(rows, TOPK, model)  10 us
  transfers between devices with their start and end apart: 10, of which 8 were waited for; matrix products, arithmetic and copies ran while one was open for 10% of the time, Pallas kernels for 0%

profile of v1, /device:TPU:34, one launch (start us, length us, event | category | flops | bytes accessed | tf_op | source)
XLA Modules:
  0.0 471.8 jit_solution(16015862847628143762)
XLA Ops:
  15.0 9.0 %reduce-window.19 = s32[32,8,128]{2,1,0:T(8,128)S(1)} reduce-window(s32[32,8,128]{2,1,0:T(8,128)S(1)} %fusion.64, s32[]{:T(128)} %constant.81.clone.1), window={size=1x1x128 pad=0_0x0_0x127_0}, to_apply=%region_11.12 | reduce-window | flops 4161536 | bytes 262148 | tf_op jit(solution)/shard_map/reduce-window.2
  24.6 4.3 scatter_custom_fusion
  32.5 5.6 %collective-permute-done.2 = bf16[384,1536]{1,0:T(8,128)(2,1)} collective-permute-done((bf16[384,1536]{1,0:T(8,128)(2,1)}, bf16[384,1536]{1,0:T(8,128)(2,1)}, u32[]{:S(2)}, u32[]{:S(2)}) %collective-permute-start.2) | collective-permute-done | bytes 1179680 | tf_op jit(solution)/shard_map/ppermute | solution.py:27
  38.4 2.4 broadcast_in_dim.99
  40.8 2.4 constant_dynamic-update-slice_fusion.3
  43.1 2.4 constant_dynamic-update-slice_fusion.2
  45.5 2.4 constant_dynamic-update-slice_fusion.1
  47.9 40.8 %all-gather.6.cloned.1.call-done = bf16[1,512,2,512]{3,2,0,1:T(2,128)(2,1)} async-done(((bf16[1,8,2,512]{3,2,0,1:T(2,128)(2,1)}), bf16[1,512,2,512]{3,2,0,1:T(2,128)(2,1)}) %all-gather.6.cloned.1.call-update) | async-done | bytes 1048592 | tf_op jit(solution)/shard_map/all_gather | solution.py:139
  88.7 4.1 fusion.74
  92.8 3.5 copy.57
  96.3 3.5 copy.58
  99.8 2.4 constant_dynamic-update-slice_fusion
  102.2 68.9 %all-gather.4.cloned.1.call-done = bf16[1536,2560]{1,0:T(8,128)(2,1)} async-done(((bf16[1536,640]{1,0:T(8,128)(2,1)}), bf16[1536,2560]{1,0:T(8,128)(2,1)}) %all-gather.4.cloned.1.call-update) | async-done | bytes 7864336 | tf_op jit(solution)/shard_map/all_gather | solution.py:115
  171.1 4.5 convolution_convert_fusion.1
  179.8 5.7 %collective-permute-done = bf16[1,128,2,512]{3,1,2,0:T(8,128)(2,1)} collective-permute-done((bf16[1,128,2,512]{3,1,2,0:T(8,128)(2,1)}, bf16[1,128,2,512]{3,1,2,0:T(8,128)(2,1)}, u32[]{:S(2)}, u32[]{:S(2)}) %collective-permute-start) | collective-permute-done | bytes 262176 | tf_op jit(solution)/shard_map/ppermute | solution.py:47
  186.6 3.6 collective-permute-start.1
  191.2 3.7 bitcast_reduce_fusion
  194.9 6.6 %collective-permute-done.1 = bf16[2,128,2,512]{3,1,2,0:T(8,128)(2,1)S(1)} collective-permute-done((bf16[2,128,2,512]{3,1,2,0:T(8,128)(2,1)S(1)}, bf16[2,128,2,512]{3,1,2,0:T(8,128)(2,1)S(1)}, u32[]{:S(2)}, u32[]{:S(2)}) %collective-permute-start.1) | collective-permute-done | bytes 524320 | tf_op jit(solution)/shard_map/ppermute | solution.py:47
  213.6 3.2 fusion.43
  217.1 5.4 %gather_fusion = bf16[1280,1536]{1,0:T(8,128)(2,1)} fusion(bf16[129,1536]{1,0:T(8,128)(2,1)S(1)} %concatenate.40, s32[2048]{0:T(1024)S(1)} %pad_clamp_fusion), kind=kCustom, calls=%fused_computation | custom fusion | bytes 7869440 | tf_op jit(solution)/shard_map/gather | solution.py:183
  222.6 98.5 %all_to_all.10 = bf16[32,40,1536]{2,1,0:T(8,128)(2,1)S(1)} all-to-all(bf16[32,40,1536]{2,1,0:T(8,128)(2,1)} %bitcast.159), channel_id=1, replica_groups=mesh['dp'=4,'chip'=32,'core'=2] {'chip'}, dimensions={0} | all-to-all | bytes 7864320 | tf_op jit(solution)/shard_map/all_to_all | solution.py:184
  321.0 2.0 copy-done.2
  323.0 6.9 %collective-permute-done.5 = bf16[32,40,1536]{2,1,0:T(8,128)(2,1)} collective-permute-done((bf16[32,40,1536]{2,1,0:T(8,128)(2,1)S(1)}, bf16[32,40,1536]{2,1,0:T(8,128)(2,1)}, u32[]{:S(2)}, u32[]{:S(2)}) %collective-permute-start.5) | collective-permute-done | bytes 3932192 | tf_op jit(solution)/shard_map/ppermute | solution.py:185
  329.9 7.1 %pad_maximum_fusion = bf16[64,40,1536]{2,1,0:T(8,128)(2,1)} fusion(bf16[32,40,1536]{2,1,0:T(8,128)(2,1)} %collective-permute-done.5, bf16[32,40,1536]{2,1,0:T(8,128)(2,1)} %copy-done.2), kind=kLoop, calls=%fused_computation.4 | loop fusion | flops 3932160 | bytes 15728640 | tf_op jit(solution)/shard_map/concatenate | solution.py:186
  337.0 6.6 %fusion.18 = f32[2560,512]{1,0:T(8,128)S(1)} fusion(bf16[2560,1536]{1,0:T(8,128)(2,1)} %bitcast.161, bf16[1,1536,512]{2,1,0:T(8,128)(2,1)S(1)} %copy-done), kind=kOutput, calls=%fused_computation.29 | convolution fusion | flops 4026531840 | bytes 14680064 | tf_op jit(solution)/shard_map/dot_general | solution.py:187
  343.6 2.3 convolution_convert_fusion
  346.7 6.6 %collective-permute-done.6 = bf16[32,40,1536]{2,1,0:T(8,128)(2,1)S(1)} collective-permute-done((bf16[32,40,1536]{2,1,0:T(8,128)(2,1)S(1)}, bf16[32,40,1536]{2,1,0:T(8,128)(2,1)S(1)}, u32[]{:S(2)}, u32[]{:S(2)}) %collective-permute-start.6) | collective-permute-done | bytes 3932192 | tf_op jit(solution)/shard_map/ppermute | solution.py:193
  353.3 3.0 fusion
  356.3 6.0 %all-to-all-start.1 = ((bf16[32,40,1536]{2,1,0:T(8,128)(2,1)}), bf16[32,40,1536]{2,1,0:T(8,128)(2,1)}, u32[]{:S(2)}, u32[]{:S(2)}) async-start(bf16[32,40,1536]{2,1,0:T(8,128)(2,1)} %fusion), calls=%async_computation.1 | async-start | bytes 7864320 | tf_op jit(solution)/shard_map/all_to_all | solution.py:195
  362.5 88.7 %all-to-all-done.1 = bf16[32,40,1536]{2,1,0:T(8,128)(2,1)} async-done(((bf16[32,40,1536]{2,1,0:T(8,128)(2,1)}), bf16[32,40,1536]{2,1,0:T(8,128)(2,1)}, u32[]{:S(2)}, u32[]{:S(2)}) %all-to-all-start.1) | async-done | bytes 3932192 | tf_op jit(solution)/shard_map/all_to_all | solution.py:195
  451.2 10.0 %gather_fusion.1 = bf16[1024,1536]{1,0:T(8,128)(2,1)} fusion(bf16[1280,1536]{1,0:T(8,128)(2,1)} %bitcast.47, s32[1024]{0:T(1024)S(1)} %broadcast_clamp_fusion), kind=kCustom, calls=%fused_computation.1 | custom fusion | bytes 6295552 | tf_op jit(solution)/shard_map/gather | solution.py:196
  461.2 2.8 fusion.9
  (114 shorter events, 32.3 us)
Async XLA Ops:
  7.2 329.8 %copy-start = (bf16[1,1536,512]{2,1,0:T(8,128)(2,1)S(1)}, bf16[1,1536,512]{2,1,0:T(8,128)(2,1)}, u32[]{:S(2)}) copy-start(bf16[1,1536,512]{2,1,0:T(8,128)(2,1)} %param.20) | copy-start | bytes 4718596
  7.2 24.1 %copy-start.3 = (bf16[1,128,1536]{2,1,0:T(8,128)(2,1)S(1)}, bf16[1,128,1536]{2,1,0:T(8,128)(2,1)}, u32[]{:S(2)}) copy-start(bf16[1,128,1536]{2,1,0:T(8,128)(2,1)} %param.11) | copy-start | bytes 1179652
  7.2 81.5 %all-gather.6.cloned.1.call-start = ((), (), s32[]{:S(2)}) async-start(), calls=%async_computation.3 | async-start | bytes 1064960 | tf_op jit(solution)/shard_map/all_gather | solution.py:139
  7.9 163.2 %all-gather.4.cloned.1.call-start = ((), (), s32[]{:S(2)}) async-start(), calls=%async_computation.2 | async-start | bytes 9830400 | tf_op jit(solution)/shard_map/all_gather | solution.py:115
  8.7 29.4 %collective-permute-start.2 = (bf16[384,1536]{1,0:T(8,128)(2,1)}, bf16[384,1536]{1,0:T(8,128)(2,1)}, u32[]{:S(2)}, u32[]{:S(2)}) collective-permute-start(bf16[384,1536]{1,0:T(8,128)(2,1)} %param.14), channel_id=1, source_target_pairs={{0,64},{64,128},{128,192},{192,0},{1,65},{65,129},{129,193},{193,1... | collective-permute-start | bytes 3538952 | tf_op jit(solution)/shard_map/ppermute | solution.py:27
  10.3 35.2 %collective-permute-start.3 = (bf16[384,1536]{1,0:T(8,128)(2,1)}, bf16[384,1536]{1,0:T(8,128)(2,1)}, u32[]{:S(2)}, u32[]{:S(2)}) collective-permute-start(bf16[384,1536]{1,0:T(8,128)(2,1)} %param.14), channel_id=1, source_target_pairs={{0,192},{64,0},{128,64},{192,128},{1,193},{65,1},{129,65},{193,129... | collective-permute-start | bytes 3538952 | tf_op jit(solution)/shard_map/ppermute | solution.py:32
  30.8 14.7 %copy-start.9 = (f32[128,64]{0,1:T(8,128)}, f32[128,64]{0,1:T(8,128)S(1)}, u32[]{:S(2)}) copy-start(f32[128,64]{0,1:T(8,128)S(1)} %get-tuple-element.29) | copy-start | bytes 98308
  38.1 61.7 %collective-permute-start.4 = (bf16[384,1536]{1,0:T(8,128)(2,1)}, bf16[384,1536]{1,0:T(8,128)(2,1)}, u32[]{:S(2)}, u32[]{:S(2)}) collective-permute-start(bf16[384,1536]{1,0:T(8,128)(2,1)} %collective-permute-done.2), channel_id=1, source_target_pairs={{0,64},{64,128},{128,192},{192,0},{1,65},{65,129},{129,193},{193,1... | collective-permute-start | bytes 3538952 | tf_op jit(solution)/shard_map/ppermute | solution.py:27
  88.7 82.4 %copy-start.10 = (f32[1536]{0:T(1024)S(1)}, f32[1536]{0:T(1024)}, u32[]{:S(2)}) copy-start(f32[1536]{0:T(1024)} %param.12) | copy-start | bytes 18436
  177.5 8.0 %collective-permute-start = (bf16[1,128,2,512]{3,1,2,0:T(8,128)(2,1)}, bf16[1,128,2,512]{3,1,2,0:T(8,128)(2,1)}, u32[]{:S(2)}, u32[]{:S(2)}) collective-permute-start(bf16[1,128,2,512]{3,1,2,0:T(8,128)(2,1)} %maximum_bitcast_fusion), channel_id=1, source_target_pairs={{0,1},{1,2},{2,3},{3,4},{4,5},{5,6},{6,7},{7,8},{8,9},{9,10},{10,1... | collective-permute-start | bytes 786440 | tf_op jit(solution)/shard_map/ppermute | solution.py:47
  179.8 11.4 %copy-start.5 = (bf16[512,1,512]{0,2,1:T(8,128)(2,1)S(1)}, bf16[512,1,512]{0,2,1:T(8,128)(2,1)}, u32[]{:S(2)}) copy-start(bf16[512,1,512]{0,2,1:T(8,128)(2,1)} %copy.57) | copy-start | bytes 1572868
  186.6 14.9 %collective-permute-start.1 = (bf16[2,128,2,512]{3,1,2,0:T(8,128)(2,1)S(1)}, bf16[2,128,2,512]{3,1,2,0:T(8,128)(2,1)S(1)}, u32[]{:S(2)}, u32[]{:S(2)}) collective-permute-start(bf16[2,128,2,512]{3,1,2,0:T(8,128)(2,1)S(1)} %pad_maximum_fusion.2), channel_id=1, source_target_pairs={{0,2},{1,3},{2,4},{3,5},{4,6},{5,7},{6,8},{7,9},{8,10},{9,11},{10,... | collective-permute-start | bytes 1572872 | tf_op jit(solution)/shard_map/ppermute | solution.py:47
  194.9 11.0 %copy-start.6 = (pred[128,512]{0,1:T(8,128)(4,1)S(1)}, pred[128,512]{0,1:T(8,128)(4,1)}, u32[]{:S(2)}) copy-start(pred[128,512]{0,1:T(8,128)(4,1)} %compare_and_fusion) | copy-start | bytes 196612
  206.9 1.6 copy-start.8
  207.0 3.3 slice-start
  208.5 1.8 slice-start.1
  210.2 1.7 copy-start.7
  213.6 3.3 copy-start.11
  216.9 247.2 %copy-start.4 = (bf16[128,1536]{1,0:T(8,128)(2,1)}, bf16[128,1536]{1,0:T(8,128)(2,1)S(1)}, u32[]{:S(2)}) copy-start(bf16[128,1536]{1,0:T(8,128)(2,1)S(1)} %get-tuple-element.28) | copy-start | bytes 1179652
  321.0 2.0 copy-start.2
  323.0 6.9 %collective-permute-start.5 = (bf16[32,40,1536]{2,1,0:T(8,128)(2,1)S(1)}, bf16[32,40,1536]{2,1,0:T(8,128)(2,1)}, u32[]{:S(2)}, u32[]{:S(2)}) collective-permute-start(bf16[32,40,1536]{2,1,0:T(8,128)(2,1)S(1)} %all_to_all.10), channel_id=1, source_target_pairs={{0,1},{1,0},{2,3},{3,2},{4,5},{5,4},{6,7},{7,6},{8,9},{9,8},{10,11... | collective-permute-start | bytes 11796488 | tf_op jit(solution)/shard_map/ppermute | solution.py:185
  337.0 6.6 %copy-start.13 = (bf16[1,256,1536]{2,1,0:T(8,128)(2,1)S(1)}, bf16[1,256,1536]{2,1,0:T(8,128)(2,1)}, u32[]{:S(2)}) copy-start(bf16[1,256,1536]{2,1,0:T(8,128)(2,1)} %param.21) | copy-start | bytes 2359300
  346.5 6.9 %collective-permute-start.6 = (bf16[32,40,1536]{2,1,0:T(8,128)(2,1)S(1)}, bf16[32,40,1536]{2,1,0:T(8,128)(2,1)S(1)}, u32[]{:S(2)}, u32[]{:S(2)}) collective-permute-start(bf16[32,40,1536]{2,1,0:T(8,128)(2,1)S(1)} %bitcast.166), channel_id=1, source_target_pairs={{0,1},{1,0},{2,3},{3,2},{4,5},{5,4},{6,7},{7,6},{8,9},{9,8},{10,11... | collective-permute-start | bytes 11796488 | tf_op jit(solution)/shard_map/ppermute | solution.py:193
  356.3 6.0 %copy-start.12 = (f32[1,128,8]{1,2,0:T(8,128)S(1)}, f32[1,128,8]{1,2,0:T(8,128)}, u32[]{:S(2)}) copy-start(f32[1,128,8]{1,2,0:T(8,128)} %param.19) | copy-start | bytes 12292
  356.3 94.9 %all-to-all-start.1 = ((bf16[32,40,1536]{2,1,0:T(8,128)(2,1)}), bf16[32,40,1536]{2,1,0:T(8,128)(2,1)}, u32[]{:S(2)}, u32[]{:S(2)}) async-start(bf16[32,40,1536]{2,1,0:T(8,128)(2,1)} %fusion), calls=%async_computation.1 | async-start | bytes 7864320 | tf_op jit(solution)/shard_map/all_to_all | solution.py:195
  451.2 13.7 %copy-start.1 = (bf16[1,1536,512]{2,1,0:T(8,128)(2,1)S(1)}, bf16[1,1536,512]{2,1,0:T(8,128)(2,1)}, u32[]{:S(2)}) copy-start(bf16[1,1536,512]{2,1,0:T(8,128)(2,1)} %param.20) | copy-start | bytes 4718596
Sparse Core Ops, SparseCore 0:
  10.8 77.8 all-gather.5
  90.5 80.5 all-gather.3
